TPU v7x, 512 devices: a whole 4x8x8 slice. The times are simulated.
512 devices in a mesh: angle: 8 (over x, core), gx: 16 (over y, z_lo), gy: 4 (over z_hi).
Axes of the slice: x: 4, y: 8, z: 8 (z_hi: 4, z_lo: 2; z = z_hi * 2 + z_lo), core: 2. Of those that a mesh axis runs over, the one named last changes fastest.
Arguments:
- forward_fields: float32 [8, 12, 128, 64, 128], P('angle', None, 'gx', 'gy'), may hold values from -6 to 6
- adjoint_fields: float32 [8, 12, 128, 64, 128], P('angle', None, 'gx', 'gy'), may hold values from -6 to 6
- forward_spectrum: float32 [8, 6, 128, 64, 128], P('angle', None, 'gx', 'gy'), may hold values from -6 to 6
- adjoint_spectrum: float32 [8, 6, 128, 64, 128], P('angle', None, 'gx', 'gy'), may hold values from -6 to 6
- permittivity: float32 [128, 64, 128], P('gx', 'gy'), may hold values from 1 to 12
- phase_table: float32 [8, 2], replicated, may hold values from -3.140625 to 3.140625
- angle_index: int32 [8], P('angle'), may hold values from 0 to 7, each once
- design_tiles: int32 [16], replicated, may hold values from 0 to 63, as said below
Outputs:
- forward_transform: float32 [8, 6, 128, 64, 128], P('angle', None, 'gx', 'gy')
- adjoint_transform: float32 [8, 6, 128, 64, 128], P('angle', None, 'gx', 'gy')
- gradient: float32 [128, 64, 128], P('gx', 'gy', 'angle')
Inputs may be any that keep to these rules, and one draw needn't show every extreme that they name: `angle_index`: every row of phase_table is used by exactly one angle. `design_tiles`: 16 distinct tile numbers; tiles 0 and 63 are always among them.
All inputs are finite; a program needn't handle non-finite values.
Results may differ from a plain program's by a relative error of at most 0.0001.
Values sent between devices are 32-bit elements; how exact they have to be, the bound alone decides.
A program may use at most 64 MiB of HBM per device.

v0:
```python
import math

import jax
import jax.numpy as jnp
from jax import lax
from jax.sharding import PartitionSpec as P

STEPS = 3


courant = 0.5
omega_step = 0.7


def from_behind(value, axis, steps):
    count = lax.axis_size(axis)
    pairs = [(source, (source + steps) % count) for source in range(count)]
    return lax.ppermute(value, axis, pairs)


def rotate_runs(pair, cosine, sine):
    sine_full = sine.reshape((2,) + (1,) * (pair.ndim - 2))
    real_part = pair[:, 0]
    imag_part = pair[:, 1]
    return jnp.stack(
        [real_part * cosine - imag_part * sine_full, real_part * sine_full + imag_part * cosine],
        axis=1,
    )


def next_depth(field):
    return jnp.concatenate([field[..., 1:], jnp.zeros_like(field[..., :1])], axis=-1)


def prev_depth(field):
    return jnp.concatenate([jnp.zeros_like(field[..., :1]), field[..., :-1]], axis=-1)


def curl_forward(efield, phases):
    cos_x, sine_x, cos_y, sine_y = phases
    place_x = lax.axis_index("gx")
    place_y = lax.axis_index("gy")
    last_x = lax.axis_size("gx") - 1
    last_y = lax.axis_size("gy") - 1
    send_x = efield[:, :, 1:3, 0]
    got_x = from_behind(send_x, "gx", -1)
    got_x = jnp.where(place_x == last_x, rotate_runs(got_x, cos_x, sine_x), got_x)
    send_y = jnp.stack([efield[:, :, 0, :, 0], efield[:, :, 2, :, 0]], axis=2)
    got_y = from_behind(send_y, "gy", -1)
    got_y = jnp.where(place_y == last_y, rotate_runs(got_y, cos_y, sine_y), got_y)
    comp_x = efield[:, :, 0]
    comp_y = efield[:, :, 1]
    comp_z = efield[:, :, 2]
    dz_dy = jnp.concatenate([comp_z[:, :, :, 1:], got_y[:, :, 1][:, :, :, None]], axis=3) - comp_z
    dy_dz = next_depth(comp_y) - comp_y
    dx_dz = next_depth(comp_x) - comp_x
    dz_dx = jnp.concatenate([comp_z[:, :, 1:], got_x[:, :, 1][:, :, None]], axis=2) - comp_z
    dy_dx = jnp.concatenate([comp_y[:, :, 1:], got_x[:, :, 0][:, :, None]], axis=2) - comp_y
    dx_dy = jnp.concatenate([comp_x[:, :, :, 1:], got_y[:, :, 0][:, :, :, None]], axis=3) - comp_x
    return jnp.stack([dz_dy - dy_dz, dx_dz - dz_dx, dy_dx - dx_dy], axis=2)


def curl_backward(hfield, phases):
    cos_x, sine_x, cos_y, sine_y = phases
    place_x = lax.axis_index("gx")
    place_y = lax.axis_index("gy")
    send_x = hfield[:, :, 1:3, -1]
    got_x = from_behind(send_x, "gx", 1)
    got_x = jnp.where(place_x == 0, rotate_runs(got_x, cos_x, -sine_x), got_x)
    send_y = jnp.stack([hfield[:, :, 0, :, -1], hfield[:, :, 2, :, -1]], axis=2)
    got_y = from_behind(send_y, "gy", 1)
    got_y = jnp.where(place_y == 0, rotate_runs(got_y, cos_y, -sine_y), got_y)
    comp_x = hfield[:, :, 0]
    comp_y = hfield[:, :, 1]
    comp_z = hfield[:, :, 2]
    hz_below_y = jnp.concatenate([got_y[:, :, 1][:, :, :, None], comp_z[:, :, :, :-1]], axis=3)
    hx_below_y = jnp.concatenate([got_y[:, :, 0][:, :, :, None], comp_x[:, :, :, :-1]], axis=3)
    hz_below_x = jnp.concatenate([got_x[:, :, 1][:, :, None], comp_z[:, :, :-1]], axis=2)
    hy_below_x = jnp.concatenate([got_x[:, :, 0][:, :, None], comp_y[:, :, :-1]], axis=2)
    first = comp_z - hz_below_y - (comp_y - prev_depth(comp_y))
    second = comp_x - prev_depth(comp_x) - (comp_z - hz_below_x)
    third = comp_y - hy_below_x - (comp_x - hx_below_y)
    return jnp.stack([first, second, third], axis=2)


def shards(
    forward_fields,
    adjoint_fields,
    forward_spectrum,
    adjoint_spectrum,
    permittivity,
    phase_table,
    angle_index,
    design_tiles,
):
    cells = forward_fields.shape[2:]
    fields = jnp.concatenate([forward_fields, adjoint_fields], axis=0)
    spectrum = jnp.concatenate([forward_spectrum, adjoint_spectrum], axis=0).reshape(
        (2, 2, 3) + cells
    )
    table_rows = phase_table.shape[0]
    picked = (jnp.arange(table_rows) == angle_index[0]).astype(jnp.float32)
    angle_x = jnp.sum(picked * phase_table[:, 0])
    angle_y = jnp.sum(picked * phase_table[:, 1])
    run_sign = jnp.array([1.0, -1.0], jnp.float32)
    efield = fields[:, 0:6].reshape((2, 2, 3) + cells)
    hfield = fields[:, 6:12].reshape((2, 2, 3) + cells)
    phases = (
        jnp.cos(angle_x),
        run_sign * jnp.sin(angle_x),
        jnp.cos(angle_y),
        run_sign * jnp.sin(angle_y),
    )
    coef = courant / permittivity
    for step in range(STEPS):
        hfield = hfield - courant * curl_forward(efield, phases)
        efield = efield + coef * curl_backward(hfield, phases)
        theta = omega_step * (step + 1)
        spectrum = spectrum + rotate_runs(
            efield, math.cos(theta), jnp.full((2,), math.sin(theta), jnp.float32)
        )
    local_term = jnp.sum(spectrum[0, 0] * spectrum[1, 0] - spectrum[0, 1] * spectrum[1, 1], axis=0)
    own_tile = lax.axis_index("gx") * lax.axis_size("gy") + lax.axis_index("gy")
    chosen = jnp.any(design_tiles == own_tile)
    local_term = jnp.where(chosen, local_term, jnp.zeros_like(local_term))
    groups = lax.axis_size("angle")
    whole = lax.psum(local_term, "angle")
    share = whole.shape[2] // groups
    summed = lax.dynamic_slice_in_dim(whole, lax.axis_index("angle") * share, share, 2)
    gradient = summed * (1.0 / groups)
    forward_out = spectrum[0].reshape((1, 6) + cells)
    adjoint_out = spectrum[1].reshape((1, 6) + cells)
    return (forward_out, adjoint_out, gradient)


def solution(mesh):
    in_specs = (
        P("angle", None, "gx", "gy", None),
        P("angle", None, "gx", "gy", None),
        P("angle", None, "gx", "gy", None),
        P("angle", None, "gx", "gy", None),
        P("gx", "gy", None),
        P(),
        P("angle"),
        P(),
    )
    out_specs = (
        P("angle", None, "gx", "gy", None),
        P("angle", None, "gx", "gy", None),
        P("gx", "gy", "angle"),
    )
    return jax.shard_map(shards, mesh=mesh, in_specs=in_specs, out_specs=out_specs, check_vma=False)
```

profile of v0, /device:TPU:1, one launch (start us, length us, event | category | flops | bytes accessed | tf_op | source)
XLA Modules:
  0.0 201.2 jit_solution(371373391882974185)
XLA Ops:
  7.2 1.3 constant_dynamic-update-slice_fusion.1
  8.8 0.6 pad_maximum_fusion.1
  9.4 11.6 %collective-permute-start = (f32[2,2,2,8,128]{4,1,0,3,2:T(2,128)}, f32[2,2,2,8,128]{4,1,0,3,2:T(2,128)}, u32[]{:S(2)}, u32[]{:S(2)}) collective-permute-start(f32[2,2,2,8,128]{4,1,0,3,2:T(2,128)} %pad_maximum_fusion.1), channel_id=1, source_target_pairs={{0,3},{1,0},{2,1},{3,2},{4,7},{5,4},{6,5},{7,6},{8,11},{9,8},{10,9... | collective-permute-start | bytes 98312 | tf_op jit(solution)/shard_map/ppermute | solution.py:18
  21.0 0.6 copy.182
  21.7 0.6 slice_bitcast_fusion.25
  22.3 6.0 %collective-permute-start.1 = (f32[2,2,2,16,128]{4,1,0,3,2:T(2,128)}, f32[2,2,2,16,128]{4,1,0,3,2:T(2,128)S(1)}, u32[]{:S(2)}, u32[]{:S(2)}) collective-permute-start(f32[2,2,2,16,128]{4,1,0,3,2:T(2,128)} %slice_bitcast_fusion.25), channel_id=1, source_target_pairs={{0,60},{4,0},{8,4},{12,8},{16,12},{20,16},{24,20},{28,24},{32,28},... | collective-permute-start | bytes 196616 | tf_op jit(solution)/shard_map/ppermute | solution.py:18
  29.1 0.6 fusion.48
  31.0 1.1 copy_bitcast_fusion.2
  32.1 0.8 slice_bitcast_fusion.14
  32.9 0.7 slice_bitcast_fusion.8
  33.6 0.9 broadcast_divide_fusion
  34.5 1.2 pad_maximum_fusion
  35.7 0.7 fusion.50
  36.3 1.4 compare_reduce_fusion
  39.0 2.0 %slice.554 = f32[2,2,8,16,127]{4,1,0,3,2:T(2,128)} slice(f32[2,2,8,16,128]{4,1,0,3,2:T(2,128)} %copy-done.4), slice={[0:2], [0:2], [0:8], [0:16], [1:128]} | slice | bytes 520192 | tf_op jit(solution)/shard_map/slice | solution.py:32
  41.0 1.7 slice.547
  42.7 1.6 slice.557
  44.3 1.0 slice.556
  45.4 1.0 multiply_subtract_fusion.14
  46.4 0.8 maximum_select_fusion.6
  47.4 1.4 fusion.11
  48.9 0.7 fusion.7
  49.7 0.9 fusion
  50.8 1.9 collective-permute-start.3
  52.7 1.9 collective-permute-start.2
  54.7 5.1 %collective-permute-done.2 = f32[2,2,2,8,128]{4,1,0,3,2:T(2,128)S(1)} collective-permute-done((f32[2,2,2,8,128]{4,1,0,3,2:T(2,128)S(1)}, f32[2,2,2,8,128]{4,1,0,3,2:T(2,128)S(1)}, u32[]{:S(2)}, u32[]{:S(2)}) %collective-permute-start.2) | collective-permute-done | bytes 32800 | tf_op jit(solution)/shard_map/ppermute | solution.py:18
  60.2 0.4 slice_bitcast_fusion.2
  60.6 0.8 fusion.14
  61.4 0.8 fusion.1
  62.5 1.1 multiply_subtract_fusion.2
  63.7 1.9 collective-permute-start.4
  66.3 5.4 %collective-permute-start.5 = (f32[2,2,2,16,128]{4,1,0,3,2:T(2,128)S(1)}, f32[2,2,2,16,128]{4,1,0,3,2:T(2,128)S(1)}, u32[]{:S(2)}, u32[]{:S(2)}) collective-permute-start(f32[2,2,2,16,128]{4,1,0,3,2:T(2,128)S(1)} %slice_bitcast_fusion.23), channel_id=1, source_target_pairs={{0,60},{4,0},{8,4},{12,8},{16,12},{20,16},{24,20},{28,24},{32,28},... | collective-permute-start | bytes 196616 | tf_op jit(solution)/shard_map/ppermute | solution.py:18
  71.9 1.0 collective-permute-done.5
  73.1 0.4 slice_bitcast_fusion.1
  73.5 0.6 fusion.21
  74.1 0.6 maximum_multiply_fusion.2
  74.7 0.9 copy_subtract_fusion.1
  75.9 4.3 %collective-permute-start.6 = (f32[2,2,2,8,128]{4,3,2,1,0:T(8,128)S(1)}, f32[2,2,2,8,128]{4,3,2,1,0:T(8,128)S(1)}, u32[]{:S(2)}, u32[]{:S(2)}) collective-permute-start(f32[2,2,2,8,128]{4,3,2,1,0:T(8,128)S(1)} %pad_maximum_fusion.4), channel_id=1, source_target_pairs={{0,1},{1,2},{2,3},{3,0},{4,5},{5,6},{6,7},{7,4},{8,9},{9,10},{10,1... | collective-permute-start | bytes 98312 | tf_op jit(solution)/shard_map/ppermute | solution.py:18
  80.2 1.9 collective-permute-start.7
  82.8 4.8 %collective-permute-done.7 = f32[2,2,2,16,128]{4,1,0,3,2:T(2,128)S(1)} collective-permute-done((f32[2,2,2,16,128]{4,1,0,3,2:T(2,128)S(1)}, f32[2,2,2,16,128]{4,1,0,3,2:T(2,128)S(1)}, u32[]{:S(2)}, u32[]{:S(2)}) %collective-permute-start.7) | collective-permute-done | bytes 65568 | tf_op jit(solution)/shard_map/ppermute | solution.py:18
  88.2 0.8 fusion.28
  89.0 1.1 fusion.4
  90.3 1.1 multiply_subtract_fusion.1
  91.5 3.1 %collective-permute-start.8 = (f32[2,2,2,8,128]{4,1,0,3,2:T(2,128)S(1)}, f32[2,2,2,8,128]{4,1,0,3,2:T(2,128)S(1)}, u32[]{:S(2)}, u32[]{:S(2)}) collective-permute-start(f32[2,2,2,8,128]{4,1,0,3,2:T(2,128)S(1)} %pad_maximum_fusion.5), channel_id=1, source_target_pairs={{0,3},{1,0},{2,1},{3,2},{4,7},{5,4},{6,5},{7,6},{8,11},{9,8},{10,9... | collective-permute-start | bytes 98312 | tf_op jit(solution)/shard_map/ppermute | solution.py:18
  95.4 3.6 %collective-permute-start.9 = (f32[2,2,2,16,128]{4,1,0,3,2:T(2,128)S(1)}, f32[2,2,2,16,128]{4,1,0,3,2:T(2,128)S(1)}, u32[]{:S(2)}, u32[]{:S(2)}) collective-permute-start(f32[2,2,2,16,128]{4,1,0,3,2:T(2,128)S(1)} %slice_bitcast_fusion.22), channel_id=1, source_target_pairs={{0,60},{4,0},{8,4},{12,8},{16,12},{20,16},{24,20},{28,24},{32,28},... | collective-permute-start | bytes 196616 | tf_op jit(solution)/shard_map/ppermute | solution.py:18
  99.2 1.2 collective-permute-done.9
  101.0 0.6 fusion.34
  101.6 0.4 maximum_multiply_fusion.4
  102.1 0.5 copy_subtract_fusion
  102.9 3.1 %collective-permute-start.10 = (f32[2,2,2,8,128]{4,3,2,1,0:T(8,128)S(1)}, f32[2,2,2,8,128]{4,3,2,1,0:T(8,128)S(1)}, u32[]{:S(2)}, u32[]{:S(2)}) collective-permute-start(f32[2,2,2,8,128]{4,3,2,1,0:T(8,128)S(1)} %copy.222), channel_id=1, source_target_pairs={{0,1},{1,2},{2,3},{3,0},{4,5},{5,6},{6,7},{7,4},{8,9},{9,10},{10,1... | collective-permute-start | bytes 98312 | tf_op jit(solution)/shard_map/ppermute | solution.py:18
  106.0 2.1 %collective-permute-start.11 = (f32[2,2,2,16,128]{4,1,0,3,2:T(2,128)S(1)}, f32[2,2,2,16,128]{4,1,0,3,2:T(2,128)S(1)}, u32[]{:S(2)}, u32[]{:S(2)}) collective-permute-start(f32[2,2,2,16,128]{4,1,0,3,2:T(2,128)S(1)} %bitcast.364), channel_id=1, source_target_pairs={{0,4},{4,8},{8,12},{12,16},{16,20},{20,24},{24,28},{28,32},{32,36}... | collective-permute-start | bytes 196616 | tf_op jit(solution)/shard_map/ppermute | solution.py:18
  108.5 1.2 collective-permute-done.10
  109.8 3.6 %collective-permute-done.11 = f32[2,2,2,16,128]{4,1,0,3,2:T(2,128)S(1)} collective-permute-done((f32[2,2,2,16,128]{4,1,0,3,2:T(2,128)S(1)}, f32[2,2,2,16,128]{4,1,0,3,2:T(2,128)S(1)}, u32[]{:S(2)}, u32[]{:S(2)}) %collective-permute-start.11) | collective-permute-done | bytes 65568 | tf_op jit(solution)/shard_map/ppermute | solution.py:18
  114.0 0.8 fusion.41
  114.8 1.3 fusion.5
  116.1 1.1 multiply_subtract_fusion
  117.2 2.4 %fusion.3 = f32[2,2,3,8,16,128]{5,1,0,4,2,3:T(2,128)S(1)} fusion(f32[2,1,3,8,16,128]{5,1,0,4,2,3:T(1,128)S(1)} %get-tuple-element.40, f32[2,1,3,8,16,128]{5,1,0,4,2,3:T(1,128)S(1)} %get-tuple-element.39, f32[2,1,3,8,16,128]{5,1,0,4,2,3:T(1,128)S(1)} %get-tuple-element.25, f32[2,1,3,8,16,128]{5,1,0,4,2,3:T(1,128)S(1)} %get-tuple-element.24, ...), kind=kLoop, calls=%fused_computation.7 | loop fusion | flops 1179648 | bytes 3932160 | tf_op jit(solution)/shard_map/add | solution.py:119
  119.5 0.6 fusion.47
  120.1 1.3 broadcast_select_fusion
  121.4 0.4 fusion.53
  121.8 0.8 copy.232
  122.6 0.8 copy.233
  123.4 69.4 %all-reduce.14.cloned.1.call-done = f32[8,16,128]{2,1,0:T(8,128)} async-done(((f32[8,16,128]{2,1,0:T(8,128)}), f32[8,16,128]{2,1,0:T(8,128)}) %all-reduce.14.cloned.1.call-update) | async-done | bytes 65552 | tf_op jit(solution)/shard_map/psum | solution.py:127
  192.8 1.6 dynamic-slice_multiply_fusion
  (128 shorter events, 7.2 us)
Async XLA Ops:
  7.2 1.4 copy-start.9
  7.2 185.6 %all-reduce.14.cloned.1.call-start = ((), (), s32[]{:S(2)}) async-start(), calls=%async_computation | async-start | bytes 131072 | tf_op jit(solution)/shard_map/psum | solution.py:127
  9.4 19.6 %copy-start.10 = (f32[8,2]{0,1:T(2,128)S(1)}, f32[8,2]{0,1:T(2,128)}, u32[]{:S(2)}) copy-start(f32[8,2]{0,1:T(2,128)} %param.14) | copy-start | bytes 196
  9.4 36.0 %collective-permute-start = (f32[2,2,2,8,128]{4,1,0,3,2:T(2,128)}, f32[2,2,2,8,128]{4,1,0,3,2:T(2,128)}, u32[]{:S(2)}, u32[]{:S(2)}) collective-permute-start(f32[2,2,2,8,128]{4,1,0,3,2:T(2,128)} %pad_maximum_fusion.1), channel_id=1, source_target_pairs={{0,3},{1,0},{2,1},{3,2},{4,7},{5,4},{6,5},{7,6},{8,11},{9,8},{10,9... | collective-permute-start | bytes 98312 | tf_op jit(solution)/shard_map/ppermute | solution.py:18
  22.3 24.9 %collective-permute-start.1 = (f32[2,2,2,16,128]{4,1,0,3,2:T(2,128)}, f32[2,2,2,16,128]{4,1,0,3,2:T(2,128)S(1)}, u32[]{:S(2)}, u32[]{:S(2)}) collective-permute-start(f32[2,2,2,16,128]{4,1,0,3,2:T(2,128)} %slice_bitcast_fusion.25), channel_id=1, source_target_pairs={{0,60},{4,0},{8,4},{12,8},{16,12},{20,16},{24,20},{28,24},{32,28},... | collective-permute-start | bytes 196616 | tf_op jit(solution)/shard_map/ppermute | solution.py:18
  28.3 5.3 %copy-start = (f32[2,2,1,8,16,128]{5,4,3,2,1,0:T(8,128)}, f32[2,2,1,8,16,128]{5,4,3,2,1,0:T(8,128)S(1)}, u32[]{:S(2)}) copy-start(f32[2,2,1,8,16,128]{5,4,3,2,1,0:T(8,128)S(1)} %get-tuple-element.49) | copy-start | bytes 786436
  28.4 5.2 %copy-start.2 = (f32[2,2,8,16,128]{4,1,0,3,2:T(2,128)}, f32[2,2,8,16,128]{4,1,0,3,2:T(2,128)S(1)}, u32[]{:S(2)}) copy-start(f32[2,2,8,16,128]{4,1,0,3,2:T(2,128)S(1)} %slice_bitcast_fusion.21) | copy-start | bytes 786436
  32.1 1.5 copy-start.4
  39.0 5.3 %copy-start.3 = (f32[2,2,8,16,128]{4,1,0,3,2:T(2,128)S(1)}, f32[2,2,8,16,128]{4,1,0,3,2:T(2,128)}, u32[]{:S(2)}) copy-start(f32[2,2,8,16,128]{4,1,0,3,2:T(2,128)} %copy-done.2) | copy-start | bytes 786436
  45.4 3.5 %copy-start.1 = (f32[2,2,1,8,16,128]{5,4,3,2,1,0:T(8,128)S(1)}, f32[2,2,1,8,16,128]{5,4,3,2,1,0:T(8,128)}, u32[]{:S(2)}) copy-start(f32[2,2,1,8,16,128]{5,4,3,2,1,0:T(8,128)} %copy-done) | copy-start | bytes 786436
  45.4 3.5 %copy-start.5 = (f32[2,2,8,16,127]{4,1,0,3,2:T(2,128)S(1)}, f32[2,2,8,16,127]{4,1,0,3,2:T(2,128)}, u32[]{:S(2)}) copy-start(f32[2,2,8,16,127]{4,1,0,3,2:T(2,128)} %slice.554) | copy-start | bytes 780292
  45.4 3.5 %copy-start.6 = (f32[2,2,8,16,127]{4,1,0,3,2:T(2,128)S(1)}, f32[2,2,8,16,127]{4,1,0,3,2:T(2,128)}, u32[]{:S(2)}) copy-start(f32[2,2,8,16,127]{4,1,0,3,2:T(2,128)} %slice.556) | copy-start | bytes 780292
  45.4 3.5 %copy-start.7 = (f32[2,2,8,15,128]{4,1,0,3,2:T(2,128)S(1)}, f32[2,2,8,15,128]{4,1,0,3,2:T(2,128)}, u32[]{:S(2)}) copy-start(f32[2,2,8,15,128]{4,1,0,3,2:T(2,128)} %slice.547) | copy-start | bytes 737284
  45.4 3.5 %copy-start.8 = (f32[2,2,7,16,128]{4,1,0,3,2:T(2,128)S(1)}, f32[2,2,7,16,128]{4,1,0,3,2:T(2,128)}, u32[]{:S(2)}) copy-start(f32[2,2,7,16,128]{4,1,0,3,2:T(2,128)} %slice.557) | copy-start | bytes 688132
  50.8 9.2 %collective-permute-start.3 = (f32[2,2,2,16,128]{4,1,0,3,2:T(2,128)S(1)}, f32[2,2,2,16,128]{4,1,0,3,2:T(2,128)S(1)}, u32[]{:S(2)}, u32[]{:S(2)}) collective-permute-start(f32[2,2,2,16,128]{4,1,0,3,2:T(2,128)S(1)} %slice_bitcast_fusion.24), channel_id=1, source_target_pairs={{0,4},{4,8},{8,12},{12,16},{16,20},{20,24},{24,28},{28,32},{32,36}... | collective-permute-start | bytes 196616 | tf_op jit(solution)/shard_map/ppermute | solution.py:18
  52.7 7.1 %collective-permute-start.2 = (f32[2,2,2,8,128]{4,1,0,3,2:T(2,128)S(1)}, f32[2,2,2,8,128]{4,1,0,3,2:T(2,128)S(1)}, u32[]{:S(2)}, u32[]{:S(2)}) collective-permute-start(f32[2,2,2,8,128]{4,1,0,3,2:T(2,128)S(1)} %pad_maximum_fusion.2), channel_id=1, source_target_pairs={{0,1},{1,2},{2,3},{3,0},{4,5},{5,6},{6,7},{7,4},{8,9},{9,10},{10,1... | collective-permute-start | bytes 98312 | tf_op jit(solution)/shard_map/ppermute | solution.py:18
  63.7 8.1 %collective-permute-start.4 = (f32[2,2,2,8,128]{4,1,0,3,2:T(2,128)S(1)}, f32[2,2,2,8,128]{4,1,0,3,2:T(2,128)S(1)}, u32[]{:S(2)}, u32[]{:S(2)}) collective-permute-start(f32[2,2,2,8,128]{4,1,0,3,2:T(2,128)S(1)} %pad_maximum_fusion.3), channel_id=1, source_target_pairs={{0,3},{1,0},{2,1},{3,2},{4,7},{5,4},{6,5},{7,6},{8,11},{9,8},{10,9... | collective-permute-start | bytes 98312 | tf_op jit(solution)/shard_map/ppermute | solution.py:18
  66.3 6.5 %collective-permute-start.5 = (f32[2,2,2,16,128]{4,1,0,3,2:T(2,128)S(1)}, f32[2,2,2,16,128]{4,1,0,3,2:T(2,128)S(1)}, u32[]{:S(2)}, u32[]{:S(2)}) collective-permute-start(f32[2,2,2,16,128]{4,1,0,3,2:T(2,128)S(1)} %slice_bitcast_fusion.23), channel_id=1, source_target_pairs={{0,60},{4,0},{8,4},{12,8},{16,12},{20,16},{24,20},{28,24},{32,28},... | collective-permute-start | bytes 196616 | tf_op jit(solution)/shard_map/ppermute | solution.py:18
  75.9 6.8 %collective-permute-start.6 = (f32[2,2,2,8,128]{4,3,2,1,0:T(8,128)S(1)}, f32[2,2,2,8,128]{4,3,2,1,0:T(8,128)S(1)}, u32[]{:S(2)}, u32[]{:S(2)}) collective-permute-start(f32[2,2,2,8,128]{4,3,2,1,0:T(8,128)S(1)} %pad_maximum_fusion.4), channel_id=1, source_target_pairs={{0,1},{1,2},{2,3},{3,0},{4,5},{5,6},{6,7},{7,4},{8,9},{9,10},{10,1... | collective-permute-start | bytes 98312 | tf_op jit(solution)/shard_map/ppermute | solution.py:18
  80.2 7.5 %collective-permute-start.7 = (f32[2,2,2,16,128]{4,1,0,3,2:T(2,128)S(1)}, f32[2,2,2,16,128]{4,1,0,3,2:T(2,128)S(1)}, u32[]{:S(2)}, u32[]{:S(2)}) collective-permute-start(f32[2,2,2,16,128]{4,1,0,3,2:T(2,128)S(1)} %bitcast.365), channel_id=1, source_target_pairs={{0,4},{4,8},{8,12},{12,16},{16,20},{20,24},{24,28},{28,32},{32,36}... | collective-permute-start | bytes 196616 | tf_op jit(solution)/shard_map/ppermute | solution.py:18
  91.5 7.5 %collective-permute-start.8 = (f32[2,2,2,8,128]{4,1,0,3,2:T(2,128)S(1)}, f32[2,2,2,8,128]{4,1,0,3,2:T(2,128)S(1)}, u32[]{:S(2)}, u32[]{:S(2)}) collective-permute-start(f32[2,2,2,8,128]{4,1,0,3,2:T(2,128)S(1)} %pad_maximum_fusion.5), channel_id=1, source_target_pairs={{0,3},{1,0},{2,1},{3,2},{4,7},{5,4},{6,5},{7,6},{8,11},{9,8},{10,9... | collective-permute-start | bytes 98312 | tf_op jit(solution)/shard_map/ppermute | solution.py:18
  95.4 5.0 %collective-permute-start.9 = (f32[2,2,2,16,128]{4,1,0,3,2:T(2,128)S(1)}, f32[2,2,2,16,128]{4,1,0,3,2:T(2,128)S(1)}, u32[]{:S(2)}, u32[]{:S(2)}) collective-permute-start(f32[2,2,2,16,128]{4,1,0,3,2:T(2,128)S(1)} %slice_bitcast_fusion.22), channel_id=1, source_target_pairs={{0,60},{4,0},{8,4},{12,8},{16,12},{20,16},{24,20},{28,24},{32,28},... | collective-permute-start | bytes 196616 | tf_op jit(solution)/shard_map/ppermute | solution.py:18
  102.9 6.8 %collective-permute-start.10 = (f32[2,2,2,8,128]{4,3,2,1,0:T(8,128)S(1)}, f32[2,2,2,8,128]{4,3,2,1,0:T(8,128)S(1)}, u32[]{:S(2)}, u32[]{:S(2)}) collective-permute-start(f32[2,2,2,8,128]{4,3,2,1,0:T(8,128)S(1)} %copy.222), channel_id=1, source_target_pairs={{0,1},{1,2},{2,3},{3,0},{4,5},{5,6},{6,7},{7,4},{8,9},{9,10},{10,1... | collective-permute-start | bytes 98312 | tf_op jit(solution)/shard_map/ppermute | solution.py:18
  106.0 7.4 %collective-permute-start.11 = (f32[2,2,2,16,128]{4,1,0,3,2:T(2,128)S(1)}, f32[2,2,2,16,128]{4,1,0,3,2:T(2,128)S(1)}, u32[]{:S(2)}, u32[]{:S(2)}) collective-permute-start(f32[2,2,2,16,128]{4,1,0,3,2:T(2,128)S(1)} %bitcast.364), channel_id=1, source_target_pairs={{0,4},{4,8},{8,12},{12,16},{16,20},{20,24},{24,28},{28,32},{32,36}... | collective-permute-start | bytes 196616 | tf_op jit(solution)/shard_map/ppermute | solution.py:18
Sparse Core Ops, SparseCore 0:
  121.5 71.2 all-reduce.13
where the time goes:
time: 202 us; the launch traced here: 201 us
  waiting for transfers between devices  86.5 us (43%)
  starting transfers between devices  46.9 us (23%)
  other arithmetic  31.9 us (16%)
  between operations  18.4 us (9%)
  local copies, waits for them, and re-layouts  17.4 us (9%)
    psum x1, waiting for transfers between devices, shards(): whole = lax.psum(local_term, 'angle')  69.4 us
    ppermute x12, starting transfers between devices, from_behind(): return lax.ppermute(value, axis, pairs)  46.9 us
    ppermute x12, waiting for transfers between devices, from_behind(): return lax.ppermute(value, axis, pairs)  17.1 us
    sub x15, other arithmetic, rotate_runs(): real_part * cosine - imag_part * sine_full  5.45 us
    slice x6, local copies, waits for them, and re-layouts, next_depth(): field[..., 1:]  4.42 us
  transfers between devices with their start and end apart: 13, of which 8 were waited for; matrix products, arithmetic and copies ran while one was open for 11% of the time, Pallas kernels for 0%

commit v1 on v0

v1 whole, which is shorter than its diff:
```python
import math

import jax
import jax.numpy as jnp
from jax import lax
from jax.experimental import pallas as pl
from jax.experimental.pallas import tpu as pltpu
from jax.sharding import PartitionSpec as P

STEPS = 3
COURANT = 0.5
OMEGA_STEP = 0.7
CX, CY, NZ = 8, 16, 128
ROWS = 24
GROUPS = 8
CHUNK = NZ // GROUPS
MESH = pl.DeviceIdType.MESH

KINDS = ((1, -1), (-1, 1), (-1, 0), (1, 0), (0, -1), (0, 1))
CORNER_A, CORNER_B, EX_MSG, PX_MSG, EY_MSG, PY_MSG = range(6)


def rotate(pair, cosine, sine):
    real_part, imag_part = pair
    return real_part * cosine - imag_part * sine, real_part * sine + imag_part * cosine


def kernel(
    ff, af, fs, as_, perm, phase, aidx, tiles,
    ft, at, grad,
    efield, hfield, coef, permbuf, phs, packed, landed,
    sx, sy, sc, rx, ry, rc,
    load_sem, send_sem, recv_sem, gsend_sem, grecv_sem,
):
    me_a = lax.axis_index("angle")
    me_x = lax.axis_index("gx")
    me_y = lax.axis_index("gy")
    n_a, n_x, n_y = GROUPS, lax.axis_size("gx"), lax.axis_size("gy")

    def shifted(kind):
        dx, dy = KINDS[kind]
        return {"gx": lax.rem(me_x + dx + n_x, n_x), "gy": lax.rem(me_y + dy + n_y, n_y)}

    def angle_peer(offset):
        return {"angle": lax.rem(me_a + offset, n_a)}

    loads = []
    count = [0]

    def load(src, dst):
        copy = pltpu.make_async_copy(src, dst, load_sem.at[count[0]])
        count[0] += 1
        copy.start()
        return copy

    field_loads = []
    for run, src in enumerate((ff, af)):
        group = []
        for x in range(CX):
            group.append(load(src.at[0, 0:6, x], efield.at[run, :, ROWS * x : ROWS * x + CY, :]))
            group.append(
                load(src.at[0, 6:12, x], hfield.at[run, :, ROWS * (x + 1) + 8 : ROWS * (x + 1) + 8 + CY, :])
            )
        field_loads.append(group)
    perm_load = load(perm, permbuf)
    spec_loads = [load(fs, ft), load(as_, at)]

    barrier = pltpu.get_barrier_semaphore()
    for kind in range(6):
        pl.semaphore_signal(barrier, inc=1, device_id=shifted(kind), device_id_type=MESH)
    for offset in range(1, n_a):
        pl.semaphore_signal(barrier, inc=1, device_id=angle_peer(offset), device_id_type=MESH)

    zero_rows = jnp.zeros((8, NZ), jnp.float32)
    for run in range(2):
        for c in range(6):
            for x in range(CX):
                efield[run, c, ROWS * x + CY : ROWS * x + CY + 8, :] = zero_rows

    lane = lax.broadcasted_iota(jnp.int32, (CY, NZ), 1)
    not_last = lane < NZ - 1
    not_first = lane > 0

    row = aidx[0]
    for axis, (place, last) in enumerate(((me_x, n_x - 1), (me_y, n_y - 1))):
        angle = jnp.full((8, NZ), phase[axis, row], jnp.float32)
        cosine, sine = jnp.cos(angle), jnp.sin(angle)
        one, zero = jnp.ones_like(cosine), jnp.zeros_like(cosine)
        ahead = (jnp.full((8, NZ), place, jnp.int32) == last)
        behind = (jnp.full((8, NZ), place, jnp.int32) == 0)
        phs[4 * axis] = jnp.where(ahead, cosine, one)
        phs[4 * axis + 1] = jnp.where(ahead, sine, zero)
        phs[4 * axis + 2] = jnp.where(behind, cosine, one)
        phs[4 * axis + 3] = jnp.where(behind, -sine, zero)

    def phase_pair(which, run, rows):
        c = phs[2 * which, 0:1, :]
        s = phs[2 * which + 1, 0:1, :]
        s = s if run == 0 else -s
        return jnp.broadcast_to(c, (rows, NZ)), jnp.broadcast_to(s, (rows, NZ))

    def e_rows(run, c, x, start=0):
        return efield[run, c, ROWS * x + start : ROWS * x + start + CY, :]

    def h_rows(run, c, x, start=0):
        base = ROWS * (x + 1) + 8 + start
        return hfield[run, c, base : base + CY, :]

    def set_h(run, c, x, value):
        base = ROWS * (x + 1) + 8
        hfield[run, c, base : base + CY, :] = value

    def next_z(value):
        return jnp.where(not_last, pltpu.roll(value, NZ - 1, 1), 0.0)

    def prev_z(value):
        return jnp.where(not_first, pltpu.roll(value, 1, 1), 0.0)

    def make(step, run, kind):
        if kind in (CORNER_A, CORNER_B):
            src, dst = sc.at[step, run, kind], rc.at[step, run, kind]
        elif kind in (EX_MSG, PX_MSG):
            src, dst = sx.at[step, run, kind - EX_MSG], rx.at[step, run, kind - EX_MSG]
        else:
            src, dst = sy.at[step, run, kind - EY_MSG], ry.at[step, run, kind - EY_MSG]
        return pltpu.make_async_remote_copy(
            src_ref=src,
            dst_ref=dst,
            send_sem=send_sem.at[step, run, kind],
            recv_sem=recv_sem.at[step, run, kind],
            device_id=shifted(kind),
            device_id_type=MESH,
        )

    def stage_e(step, run):
        for part in range(2):
            sc[step, run, CORNER_A, part : part + 1, :] = efield[run, 3 * part, ROWS * 7 : ROWS * 7 + 1, :]
            sc[step, run, CORNER_B, part : part + 1, :] = efield[run, 3 * part + 1, 15:16, :]
            for slot, c in enumerate((1, 2)):
                sx[step, run, 0, 2 * part + slot] = e_rows(run, 3 * part + c, 0)
            for slot, c in enumerate((0, 2)):
                sy[step, run, 0, 2 * part + slot] = efield[run, 3 * part + c, pl.ds(0, CX, stride=ROWS), :]

    def h_pass(step, run):
        for x in (7, 0, 1, 2, 3, 4, 5, 6):
            for part in range(2):
                b = 3 * part
                ex, ey, ez = (e_rows(run, b + c, x) for c in range(3))
                dz_dy = e_rows(run, b + 2, x, 1) - ez
                dx_dy = e_rows(run, b, x, 1) - ex
                dy_dz = next_z(ey) - ey
                dx_dz = next_z(ex) - ex
                if x < CX - 1:
                    dz_dx = e_rows(run, b + 2, x + 1) - ez
                    dy_dx = e_rows(run, b + 1, x + 1) - ey
                else:
                    dz_dx, dy_dx = -ez, -ey
                hx = h_rows(run, b, x) - COURANT * (dz_dy - dy_dz)
                hy = h_rows(run, b + 1, x) - COURANT * (dx_dz - dz_dx)
                hz = h_rows(run, b + 2, x) - COURANT * (dy_dx - dx_dy)
                set_h(run, b, x, hx)
                set_h(run, b + 1, x, hy)
                set_h(run, b + 2, x, hz)
                if x == CX - 1:
                    sx[step, run, 1, 2 * part] = hy
                    sx[step, run, 1, 2 * part + 1] = hz
        for part in range(2):
            for slot, c in enumerate((0, 2)):
                sy[step, run, 1, 2 * part + slot] = hfield[
                    run, 3 * part + c, pl.ds(ROWS + 8 + 15, CX, stride=ROWS), :
                ]

    def receive(step, run):
        for kind in range(6):
            make(step, run, kind).wait_recv()

    last_row = lax.broadcasted_iota(jnp.int32, (CY, NZ), 0) == CY - 1
    last_x = lax.broadcasted_iota(jnp.int32, (CX, NZ), 0) == CX - 1

    def halo(step, run):
        fwd_x, fwd_y = phase_pair(0, run, CY), phase_pair(2, run, CX)
        back_x, back_y = phase_pair(1, run, CY), phase_pair(3, run, CX)
        eyx = rotate((rx[step, run, 0, 0], rx[step, run, 0, 2]), *fwd_x)
        ezx = rotate((rx[step, run, 0, 1], rx[step, run, 0, 3]), *fwd_x)
        exy = rotate((ry[step, run, 0, 0], ry[step, run, 0, 2]), *fwd_y)
        ezy = rotate((ry[step, run, 0, 1], ry[step, run, 0, 3]), *fwd_y)
        rows = pl.ds(ROWS + 8 + 15, CX, stride=ROWS)
        for part in range(2):
            b = 3 * part
            set_h(run, b + 1, 7, h_rows(run, b + 1, 7) + COURANT * ezx[part])
            set_h(run, b + 2, 7, h_rows(run, b + 2, 7) - COURANT * eyx[part])
            hfield[run, b, rows, :] = hfield[run, b, rows, :] - COURANT * ezy[part]
            hfield[run, b + 2, rows, :] = hfield[run, b + 2, rows, :] + COURANT * exy[part]
        one_fwd_y = phase_pair(2, run, 1)
        one_fwd_x = phase_pair(0, run, 1)
        corner_a = rotate((rc[step, run, CORNER_A, 0:1, :], rc[step, run, CORNER_A, 1:2, :]), *one_fwd_y)
        corner_b = rotate((rc[step, run, CORNER_B, 0:1, :], rc[step, run, CORNER_B, 1:2, :]), *one_fwd_x)
        pz = tuple(
            rx[step, run, 1, 2 * part + 1]
            + jnp.where(last_row, jnp.broadcast_to(COURANT * corner_a[part], (CY, NZ)), 0.0)
            for part in range(2)
        )
        py = (rx[step, run, 1, 0], rx[step, run, 1, 2])
        hy_x, hz_x = rotate(py, *back_x), rotate(pz, *back_x)
        qz = tuple(
            ry[step, run, 1, 2 * part + 1]
            - jnp.where(last_x, jnp.broadcast_to(COURANT * corner_b[part], (CX, NZ)), 0.0)
            for part in range(2)
        )
        qx = (ry[step, run, 1, 0], ry[step, run, 1, 2])
        hx_y, hz_y = rotate(qx, *back_y), rotate(qz, *back_y)
        before = pl.ds(ROWS + 7, CX, stride=ROWS)
        first = pl.ds(0, CX, stride=ROWS)
        for part in range(2):
            b = 3 * part
            set_h(run, b + 1, -1, hy_x[part] + COURANT * e_rows(run, b + 2, 0))
            set_h(run, b + 2, -1, hz_x[part] - COURANT * e_rows(run, b + 1, 0))
            hfield[run, b, before, :] = hx_y[part] - COURANT * efield[run, b + 2, first, :]
            hfield[run, b + 2, before, :] = hz_y[part] + COURANT * efield[run, b, first, :]

    def e_pass(run):
        for x in range(CX):
            k = coef[x]
            for part in range(2):
                b = 3 * part
                hx, hy, hz = (h_rows(run, b + c, x) for c in range(3))
                cx = (hz - h_rows(run, b + 2, x, -1)) - (hy - prev_z(hy))
                cy = (hx - prev_z(hx)) - (hz - h_rows(run, b + 2, x - 1))
                cz = (hy - h_rows(run, b + 1, x - 1)) - (hx - h_rows(run, b, x, -1))
                for c, curl in enumerate((cx, cy, cz)):
                    efield[run, b + c, ROWS * x : ROWS * x + CY, :] = e_rows(run, b + c, x) + k * curl

    outs = (ft, at)

    def spectrum(step, run):
        theta = OMEGA_STEP * (step + 1)
        cw, sw = math.cos(theta), math.sin(theta)
        out = outs[run]
        for x in range(CX):
            for c in range(3):
                ec, es = e_rows(run, c, x), e_rows(run, 3 + c, x)
                out[0, c, x] = out[0, c, x] + (ec * cw - es * sw)
                out[0, 3 + c, x] = out[0, 3 + c, x] + (ec * sw + es * cw)

    for run in range(2):
        for copy in field_loads[run]:
            copy.wait()
        stage_e(0, run)
        h_pass(0, run)
    pl.semaphore_wait(barrier, 6 + n_a - 1)
    for run in range(2):
        for kind in range(6):
            make(0, run, kind).start()
    perm_load.wait()
    for x in range(CX):
        coef[x] = COURANT / permbuf[x]
    for copy in spec_loads:
        copy.wait()

    for step in range(STEPS):
        for run in range(2):
            receive(step, run)
            halo(step, run)
            e_pass(run)
            if step + 1 < STEPS:
                stage_e(step + 1, run)
                for kind in (CORNER_A, CORNER_B, EX_MSG, EY_MSG):
                    make(step + 1, run, kind).start()
                h_pass(step + 1, run)
                for kind in (PX_MSG, PY_MSG):
                    make(step + 1, run, kind).start()
        for run in range(2):
            spectrum(step, run)

    block = lane // CHUNK
    term = []
    for x in range(CX):
        total = None
        for c in range(3):
            value = ft[0, c, x] * at[0, c, x] - ft[0, 3 + c, x] * at[0, 3 + c, x]
            total = value if total is None else total + value
        term.append(total)
    for stride in (1, 2, 4):
        low = (block // stride) % 2 == 0
        fresh = list(term)
        for j in range(GROUPS):
            if (j // stride) % 2 == 0:
                a, b = term[j], term[j + stride]
                fresh[j] = jnp.where(low, a, pltpu.roll(b, CHUNK * stride, 1))
                fresh[j + stride] = jnp.where(low, pltpu.roll(a, NZ - CHUNK * stride, 1), b)
        term = fresh
    for j in range(GROUPS):
        packed[j] = term[j]

    def share(offset):
        peer = angle_peer(offset)
        return pltpu.make_async_remote_copy(
            src_ref=packed.at[peer["angle"]],
            dst_ref=landed.at[offset],
            send_sem=gsend_sem.at[offset],
            recv_sem=grecv_sem.at[offset],
            device_id=peer,
            device_id_type=MESH,
        )

    for offset in range(1, n_a):
        share(offset).start()
    own_tile = me_x * n_y + me_y
    hits = jnp.int32(0)
    for i in range(tiles.shape[0]):
        hits = hits + jnp.where(tiles[i] == own_tile, 1, 0)
    chosen = jnp.full((CY, NZ), hits, jnp.int32) > 0
    total = packed[me_a]
    for offset in range(1, n_a):
        share(offset).wait_recv()
        total = total + landed[offset]
    total = jnp.where(chosen, total * (1.0 / GROUPS), 0.0)
    for j in range(CX):
        moved = total if j == 0 else pltpu.roll(total, NZ - CHUNK * j, 1)
        grad[j] = moved[:, 0:CHUNK]

    for step in range(STEPS):
        for run in range(2):
            for kind in range(6):
                make(step, run, kind).wait_send()
    for offset in range(1, n_a):
        share(offset).wait_send()


def shards(ff, af, fs, as_, perm, phase_table, angle_index, design_tiles):
    f32 = jnp.float32
    hbm = pl.BlockSpec(memory_space=pl.ANY)
    smem = pl.BlockSpec(memory_space=pltpu.SMEM)
    vmem = pl.BlockSpec(memory_space=pltpu.VMEM)
    loads = 2 * 2 * CX + 3
    return pl.pallas_call(
        kernel,
        out_shape=(
            jax.ShapeDtypeStruct((1, 6, CX, CY, NZ), f32),
            jax.ShapeDtypeStruct((1, 6, CX, CY, NZ), f32),
            jax.ShapeDtypeStruct((CX, CY, CHUNK), f32),
        ),
        in_specs=[hbm] * 5 + [smem] * 3,
        out_specs=(vmem, vmem, vmem),
        scratch_shapes=[
            pltpu.VMEM((2, 6, CX * ROWS, NZ), f32),
            pltpu.VMEM((2, 6, (CX + 1) * ROWS, NZ), f32),
            pltpu.VMEM((CX, CY, NZ), f32),
            pltpu.VMEM((CX, CY, NZ), f32),
            pltpu.VMEM((8, 8, NZ), f32),
            pltpu.VMEM((GROUPS, CY, NZ), f32),
            pltpu.VMEM((GROUPS, CY, NZ), f32),
            pltpu.VMEM((STEPS, 2, 2, 4, CY, NZ), f32),
            pltpu.VMEM((STEPS, 2, 2, 4, CX, NZ), f32),
            pltpu.VMEM((STEPS, 2, 2, 2, NZ), f32),
            pltpu.VMEM((STEPS, 2, 2, 4, CY, NZ), f32),
            pltpu.VMEM((STEPS, 2, 2, 4, CX, NZ), f32),
            pltpu.VMEM((STEPS, 2, 2, 2, NZ), f32),
            pltpu.SemaphoreType.DMA((loads,)),
            pltpu.SemaphoreType.DMA((STEPS, 2, 6)),
            pltpu.SemaphoreType.DMA((STEPS, 2, 6)),
            pltpu.SemaphoreType.DMA((GROUPS,)),
            pltpu.SemaphoreType.DMA((GROUPS,)),
        ],
        compiler_params=pltpu.CompilerParams(collective_id=0, has_side_effects=True),
        name="fdtd",
    )(ff, af, fs, as_, perm, phase_table.T, angle_index, design_tiles)


def solution(mesh):
    in_specs = (
        P("angle", None, "gx", "gy", None),
        P("angle", None, "gx", "gy", None),
        P("angle", None, "gx", "gy", None),
        P("angle", None, "gx", "gy", None),
        P("gx", "gy", None),
        P(),
        P("angle"),
        P(),
    )
    out_specs = (
        P("angle", None, "gx", "gy", None),
        P("angle", None, "gx", "gy", None),
        P("gx", "gy", "angle"),
    )
    return jax.shard_map(shards, mesh=mesh, in_specs=in_specs, out_specs=out_specs, check_vma=False)
```

time: 202 us -> 44.2 us (0.22)
  waiting for transfers between devices: 86.5 us -> 0 us
  starting transfers between devices: 46.9 us -> 0 us
  Pallas kernels: 0 us -> 39.4 us
  other arithmetic: 31.9 us -> 0 us
  between operations: 18.4 us -> 1.3 us
  local copies, waits for them, and re-layouts: 17.4 us -> 3.32 us
    psum x1 -> x0, waiting for transfers between devices: 69.4 us -> none  [shards(): whole = lax.psum(local_term, 'angle')]
    ppermute x12 -> x0, starting transfers between devices: 46.9 us -> none  [from_behind(): return lax.ppermute(value, axis, pairs)]
    pallas_call x0 -> x1, Pallas kernels: none -> 39.4 us  [shards(): pl.pallas_call(kernel, out_shape=(jax.ShapeDtypeStruct((1, 6, CX, CY, NZ)...]
    ppermute x12 -> x0, waiting for transfers between devices: 17.1 us -> none  [from_behind(): return lax.ppermute(value, axis, pairs)]
    slice x34 -> x0, local copies, waits for them, and re-layouts: 10.3 us -> none  [the longest x6 4.42 us: next_depth(): field[..., 1:]]
    sub x21 -> x0, other arithmetic: 9.78 us -> none  [the longest x15 5.45 us: rotate_runs(): real_part * cosine - imag_part * sine_full]
    add x4 -> x0, other arithmetic: 5.53 us -> none  [the longest x3 3.17 us: shards(): efield = efield + coef * curl_backward(hfield, phases)]
    another operation x12 -> x0, other arithmetic: 4.96 us -> none  [the longest x3 2.38 us: curl_backward(): return jnp.stack([first, second, third], axis=2)]
  transfers between devices with their start and end apart: 13 -> 0, of which waited for: 8 -> 0; matrix products, arithmetic and copies ran while one was open for 11% -> 0% of each run, Pallas kernels for 0% -> 0%
where the time goes in v1:
time: 44.2 us; the launch traced here: 44 us
  Pallas kernels  39.4 us (89%)
  local copies, waits for them, and re-layouts  3.32 us (8%)
  between operations  1.3 us (3%)
    pallas_call x1, Pallas kernels, shards(): pl.pallas_call(kernel, out_shape=(jax.ShapeDtypeStruct((1, 6, CX, CY, NZ)...  39.4 us
    unnamed x7, local copies, waits for them, and re-layouts  3.32 us

profile of v1, /device:TPU:1, one launch (start us, length us, event | category | flops | bytes accessed | tf_op | source)
XLA Modules:
  0.0 44.0 jit_solution(13501285975512820327)
XLA Ops:
  1.3 39.4 %fdtd.1 = (f32[1,6,8,16,128]{4,3,2,1,0:T(8,128)}, f32[1,6,8,16,128]{4,3,2,1,0:T(8,128)}, f32[8,16,16]{2,1,0:T(8,128)}) custom-call(f32[1,12,8,16,128]{4,3,2,1,0:T(8,128)} %ff.1, f32[1,12,8,16,128]{4,3,2,1,0:T(8,128)} %af.1, f32[1,6,8,16,128]{4,3,2,1,0:T(8,128)} %fs.1, f32[1,6,8,16,128]{4,3,2,1,0:T(8,128)} %as_.1, f32[8,16,128]{2,1,0:T(8,128)} %perm.1, ...), custom_call_target="tpu_custom_call" | custom-call | tf_op jit(solution)/shard_map/fdtd/pallas_call | solution.py:336
  40.6 0.0 copy-start
  40.7 1.8 %copy.15 = f32[1,6,8,16,128]{4,3,2,1,0:T(8,128)} copy(f32[1,6,8,16,128]{4,3,2,1,0:T(8,128)} %get-tuple-element.6) | data formatting | bytes 786432
  42.5 0.0 copy-done
  42.5 0.0 copy-start.1
  42.5 0.7 %copy.16 = f32[1,6,8,16,128]{4,3,2,1,0:T(8,128)} copy(f32[1,6,8,16,128]{4,3,2,1,0:T(8,128)S(1)} %copy-done) | data formatting | bytes 786432
  43.2 0.1 copy-done.1
  43.4 0.6 %copy.17 = f32[8,16,16]{2,1,0:T(8,128)} copy(f32[8,16,16]{2,1,0:T(8,128)S(1)} %copy-done.1) | data formatting | bytes 16384
Async XLA Ops:
  40.6 1.8 %copy-start = (f32[1,6,8,16,128]{4,3,2,1,0:T(8,128)S(1)}, f32[1,6,8,16,128]{4,3,2,1,0:T(8,128)}, u32[]{:S(2)}) copy-start(f32[1,6,8,16,128]{4,3,2,1,0:T(8,128)} %get-tuple-element.7) | copy-start | bytes 1179652
  42.5 0.9 %copy-start.1 = (f32[8,16,16]{2,1,0:T(8,128)S(1)}, f32[8,16,16]{2,1,0:T(8,128)}, u32[]{:S(2)}) copy-start(f32[8,16,16]{2,1,0:T(8,128)} %get-tuple-element.8) | copy-start | bytes 24580

commit v2 on v1

v2 whole, which is shorter than its diff:
```python
import math

import jax
import jax.numpy as jnp
from jax import lax
from jax.experimental import pallas as pl
from jax.experimental.pallas import tpu as pltpu
from jax.sharding import PartitionSpec as P

STEPS = 3
COURANT = 0.5
OMEGA_STEP = 0.7
CX, CY, NZ = 8, 16, 128
ROWS = 24
GROUPS = 8
CHUNK = NZ // GROUPS
MESH = pl.DeviceIdType.MESH
LAST = STEPS - 1

KINDS = ((1, -1), (-1, 1), (-1, 0), (1, 0), (0, -1), (0, 1))
CORNER_A, CORNER_B, EX_MSG, PX_MSG, EY_MSG, PY_MSG = range(6)
DIRECT = (EX_MSG, PX_MSG, EY_MSG, PY_MSG)
CORNERS = (CORNER_A, CORNER_B)

E_FIRST = pl.ds(0, CX, stride=ROWS)
E_LAST = pl.ds(CY - 1, CX, stride=ROWS)
E_LAST_NEXT_X = pl.ds(ROWS + CY - 1, CX, stride=ROWS)
H_LAST = pl.ds(ROWS + 8 + CY - 1, CX, stride=ROWS)
FIRST = pl.ds(0, CX, stride=CY)
FINAL = pl.ds(CY - 1, CX, stride=CY)


def rotate(pair, cosine, sine):
    real_part, imag_part = pair
    return real_part * cosine - imag_part * sine, real_part * sine + imag_part * cosine


def kernel(
    ff, af, fs, as_, perm, phase, aidx, tiles,
    ft, at, grad,
    efield, hfield, coef, phs, terms, packed, landed,
    sx, sy, sc, rx, ry, rc,
    load_sem, send_sem, recv_sem, gsend_sem, grecv_sem, ready_sem,
):
    me_a = lax.axis_index("angle")
    me_x = lax.axis_index("gx")
    me_y = lax.axis_index("gy")
    n_a, n_x, n_y = GROUPS, lax.axis_size("gx"), lax.axis_size("gy")

    def shifted(kind):
        dx, dy = KINDS[kind]
        return {"gx": lax.rem(me_x + dx + n_x, n_x), "gy": lax.rem(me_y + dy + n_y, n_y)}

    def angle_peer(offset):
        return {"angle": lax.rem(me_a + offset, n_a)}

    barrier = pltpu.get_barrier_semaphore()
    for kind in DIRECT:
        pl.semaphore_signal(barrier, inc=1, device_id=shifted(kind), device_id_type=MESH)
    for offset in range(1, n_a):
        pl.semaphore_signal(barrier, inc=1, device_id=angle_peer(offset), device_id_type=MESH)

    count = [0]

    def load(src, dst):
        copy = pltpu.make_async_copy(src, dst, load_sem.at[count[0]])
        count[0] += 1
        copy.start()
        return copy

    field_loads = []
    for run, src in enumerate((ff, af)):
        group = []
        for x in range(CX):
            group.append(load(src.at[0, 0:6, x], efield.at[run, :, ROWS * x : ROWS * x + CY, :]))
            base = ROWS * (x + 1) + 8
            group.append(load(src.at[0, 6:12, x], hfield.at[run, :, base : base + CY, :]))
        field_loads.append(group)
    perm_load = load(perm, coef)
    spec_loads = [load(fs, ft), load(as_, at)]

    zero_rows = jnp.zeros((8, NZ), jnp.float32)
    zero_plane = jnp.zeros((CY, NZ), jnp.float32)
    for run in range(2):
        for c in range(6):
            for x in range(CX):
                efield[run, c, ROWS * x + CY : ROWS * (x + 1), :] = zero_rows
                hfield[run, c, ROWS * (x + 1) : ROWS * (x + 1) + 8, :] = zero_rows
            efield[run, c, ROWS * CX : ROWS * CX + CY, :] = zero_plane
            hfield[run, c, 8 : 8 + CY, :] = zero_plane

    lane = lax.broadcasted_iota(jnp.int32, (CY, NZ), 1)
    not_last = lane < NZ - 1
    not_first = lane > 0
    row_index = lax.broadcasted_iota(jnp.int32, (CY, NZ), 0)
    x_index = lax.broadcasted_iota(jnp.int32, (CX, NZ), 0)

    row = aidx[0]
    for axis, (place, last) in enumerate(((me_x, n_x - 1), (me_y, n_y - 1))):
        angle = jnp.full((8, NZ), phase[axis, row], jnp.float32)
        cosine, sine = jnp.cos(angle), jnp.sin(angle)
        one, zero = jnp.ones_like(cosine), jnp.zeros_like(cosine)
        ahead = jnp.full((8, NZ), place, jnp.int32) == last
        behind = jnp.full((8, NZ), place, jnp.int32) == 0
        phs[4 * axis] = jnp.where(ahead, cosine, one)
        phs[4 * axis + 1] = jnp.where(ahead, sine, zero)
        phs[4 * axis + 2] = jnp.where(behind, cosine, one)
        phs[4 * axis + 3] = jnp.where(behind, -sine, zero)

    def phase_pair(which, run, rows):
        c = phs[2 * which, 0:1, :]
        s = phs[2 * which + 1, 0:1, :]
        s = s if run == 0 else -s
        return jnp.broadcast_to(c, (rows, NZ)), jnp.broadcast_to(s, (rows, NZ))

    def e_rows(run, c, x, start=0):
        return efield[run, c, ROWS * x + start : ROWS * x + start + CY, :]

    def set_e(run, c, x, value):
        efield[run, c, ROWS * x : ROWS * x + CY, :] = value

    def h_rows(run, c, x, start=0):
        base = ROWS * (x + 1) + 8 + start
        return hfield[run, c, base : base + CY, :]

    def set_h(run, c, x, value):
        base = ROWS * (x + 1) + 8
        hfield[run, c, base : base + CY, :] = value

    def next_z(value):
        return jnp.where(not_last[: value.shape[0]], pltpu.roll(value, NZ - 1, 1), 0.0)

    def prev_z(value):
        return jnp.where(not_first[: value.shape[0]], pltpu.roll(value, 1, 1), 0.0)

    def make(step, run, kind):
        if kind in CORNERS:
            src, dst = sc.at[step, run, kind], rc.at[step, run, kind]
        elif kind in (EX_MSG, PX_MSG):
            src, dst = sx.at[step, run, kind - EX_MSG], rx.at[step, run, kind - EX_MSG]
        else:
            src, dst = sy.at[step, run, kind - EY_MSG], ry.at[step, run, kind - EY_MSG]
        return pltpu.make_async_remote_copy(
            src_ref=src,
            dst_ref=dst,
            send_sem=send_sem.at[step, run, kind],
            recv_sem=recv_sem.at[step, run, kind],
            device_id=shifted(kind),
            device_id_type=MESH,
        )

    def stage_e(step, run):
        for part in range(2):
            b = 3 * part
            sc[step, run, CORNER_A, part : part + 1, :] = efield[run, b, ROWS * 7 : ROWS * 7 + 1, :]
            sc[step, run, CORNER_B, part : part + 1, :] = efield[run, b + 1, CY - 1 : CY, :]
            for slot, c in enumerate((1, 2)):
                sx[step, run, 0, 2 * part + slot] = e_rows(run, b + c, 0)
            for slot, c in enumerate((0, 2)):
                sy[step, run, 0, 2 * part + slot] = efield[run, b + c, E_FIRST, :]

    def h_value(run, part, x):
        b = 3 * part
        ex, ey, ez = (e_rows(run, b + c, x) for c in range(3))
        dz_dy = e_rows(run, b + 2, x, 1) - ez
        dx_dy = e_rows(run, b, x, 1) - ex
        dy_dz = next_z(ey) - ey
        dx_dz = next_z(ex) - ex
        dz_dx = e_rows(run, b + 2, x + 1) - ez
        dy_dx = e_rows(run, b + 1, x + 1) - ey
        hx = h_rows(run, b, x) - COURANT * (dz_dy - dy_dz)
        hy = h_rows(run, b + 1, x) - COURANT * (dx_dz - dz_dx)
        hz = h_rows(run, b + 2, x) - COURANT * (dy_dx - dx_dy)
        return hx, hy, hz

    def stage_h(step, run):
        for part in range(2):
            b = 3 * part
            ex, ey, ez = (efield[run, b + c, E_LAST, :] for c in range(3))
            ey_next = efield[run, b + 1, E_LAST_NEXT_X, :]
            hx = hfield[run, b, H_LAST, :] + COURANT * (ez + (next_z(ey) - ey))
            hz = hfield[run, b + 2, H_LAST, :] - COURANT * ((ey_next - ey) + ex)
            sy[step, run, 1, 2 * part] = hx
            sy[step, run, 1, 2 * part + 1] = hz
        for part in range(2):
            b = 3 * part
            hx, hy, hz = h_value(run, part, CX - 1)
            sx[step, run, 1, 2 * part] = hy
            sx[step, run, 1, 2 * part + 1] = hz
            for c, value in enumerate((hx, hy, hz)):
                set_h(run, b + c, CX - 1, value)

    outs = (ft, at)

    def turn(step):
        theta = OMEGA_STEP * (step + 1)
        return math.cos(theta), math.sin(theta)

    def bulk(step, run):
        for x in range(CX - 1):
            for part in range(2):
                for c, value in enumerate(h_value(run, part, x)):
                    set_h(run, 3 * part + c, x, value)
        out = outs[run]
        for x in range(CX):
            k = coef[x]
            old, new = [], []
            for part in range(2):
                b = 3 * part
                hx, hy, hz = (h_rows(run, b + c, x) for c in range(3))
                curl_x = (hz - h_rows(run, b + 2, x, -1)) - (hy - prev_z(hy))
                curl_y = (hx - prev_z(hx)) - (hz - h_rows(run, b + 2, x - 1))
                curl_z = (hy - h_rows(run, b + 1, x - 1)) - (hx - h_rows(run, b, x, -1))
                for c, curl in enumerate((curl_x, curl_y, curl_z)):
                    e = e_rows(run, b + c, x)
                    old.append(e)
                    new.append(e + k * curl)
            rows = slice(CY * x, CY * (x + 1))
            for c in range(3):
                real, imag = None, None
                if step > 0:
                    real, imag = rotate((old[c], old[3 + c]), *turn(step - 1))
                if step == LAST:
                    more = rotate((new[c], new[3 + c]), *turn(step))
                    real = more[0] if real is None else real + more[0]
                    imag = more[1] if imag is None else imag + more[1]
                if real is not None:
                    out[0, c, rows, :] = out[0, c, rows, :] + real
                    out[0, 3 + c, rows, :] = out[0, 3 + c, rows, :] + imag
            if step < LAST:
                for c in range(6):
                    set_e(run, c, x, new[c])

    def receive(step, run):
        for kind in range(6):
            make(step, run, kind).wait_recv()

    def arrive(step, run):
        fwd_x, fwd_y = phase_pair(0, run, CY), phase_pair(2, run, CX)
        back_x, back_y = phase_pair(1, run, CY), phase_pair(3, run, CX)
        one_x, one_y = phase_pair(0, run, 1), phase_pair(2, run, 1)
        eyx = rotate((rx[step, run, 0, 0], rx[step, run, 0, 2]), *fwd_x)
        ezx = rotate((rx[step, run, 0, 1], rx[step, run, 0, 3]), *fwd_x)
        exy = rotate((ry[step, run, 0, 0], ry[step, run, 0, 2]), *fwd_y)
        ezy = rotate((ry[step, run, 0, 1], ry[step, run, 0, 3]), *fwd_y)
        corner_a = rotate((rc[step, run, CORNER_A, 0:1, :], rc[step, run, CORNER_A, 1:2, :]), *one_y)
        corner_b = rotate((rc[step, run, CORNER_B, 0:1, :], rc[step, run, CORNER_B, 1:2, :]), *one_x)
        pz = tuple(
            rx[step, run, 1, 2 * part + 1]
            + jnp.where(row_index == CY - 1, jnp.broadcast_to(COURANT * corner_a[part], (CY, NZ)), 0.0)
            for part in range(2)
        )
        qz = tuple(
            ry[step, run, 1, 2 * part + 1]
            - jnp.where(x_index == CX - 1, jnp.broadcast_to(COURANT * corner_b[part], (CX, NZ)), 0.0)
            for part in range(2)
        )
        hy_x = rotate((rx[step, run, 1, 0], rx[step, run, 1, 2]), *back_x)
        hz_x = rotate(pz, *back_x)
        hx_y = rotate((ry[step, run, 1, 0], ry[step, run, 1, 2]), *back_y)
        hz_y = rotate(qz, *back_y)
        k_first, k_last = coef[0], coef[CX - 1]
        k_row_first, k_row_last = coef.reshape(CX * CY, NZ)[FIRST, :], coef.reshape(CX * CY, NZ)[FINAL, :]
        plane_last, row_last, plane_first, row_first = [], [], [], []
        for part in range(2):
            b = 3 * part
            dy_plane, dz_plane = COURANT * ezx[part], -COURANT * eyx[part]
            dx_row, dz_row = -COURANT * ezy[part], COURANT * exy[part]
            if step < LAST:
                set_h(run, b + 1, CX - 1, h_rows(run, b + 1, CX - 1) + dy_plane)
                set_h(run, b + 2, CX - 1, h_rows(run, b + 2, CX - 1) + dz_plane)
                hfield[run, b, H_LAST, :] = hfield[run, b, H_LAST, :] + dx_row
                hfield[run, b + 2, H_LAST, :] = hfield[run, b + 2, H_LAST, :] + dz_row
            dz_above = jnp.where(row_index > 0, pltpu.roll(dz_plane, 1, 0), 0.0)
            dz_before = jnp.where(x_index > 0, pltpu.roll(dz_row, 1, 0), 0.0)
            plane_last += [
                k_last * ((dz_plane - dz_above) - (dy_plane - prev_z(dy_plane))),
                -(k_last * dz_plane),
                k_last * dy_plane,
            ]
            row_last += [
                k_row_last * dz_row,
                k_row_last * ((dx_row - prev_z(dx_row)) - (dz_row - dz_before)),
                -(k_row_last * dx_row),
            ]
            hy = hy_x[part] + COURANT * sx[step, run, 0, 2 * part + 1]
            hz = hz_x[part] - COURANT * sx[step, run, 0, 2 * part]
            plane_first += [None, k_first * hz, -(k_first * hy)]
            hx = hx_y[part] - COURANT * sy[step, run, 0, 2 * part + 1]
            hz = hz_y[part] + COURANT * sy[step, run, 0, 2 * part]
            row_first += [-(k_row_first * hz), None, k_row_first * hx]
        if step < LAST:
            for c in range(6):
                set_e(run, c, CX - 1, e_rows(run, c, CX - 1) + plane_last[c])
            for c in range(6):
                if plane_first[c] is not None:
                    set_e(run, c, 0, e_rows(run, c, 0) + plane_first[c])
            for c in range(6):
                efield[run, c, E_LAST, :] = efield[run, c, E_LAST, :] + row_last[c]
            for c in range(6):
                if row_first[c] is not None:
                    efield[run, c, E_FIRST, :] = efield[run, c, E_FIRST, :] + row_first[c]
        else:
            out = outs[run]
            for rows, gains in (
                (slice(CY * (CX - 1), CY * CX), plane_last),
                (slice(0, CY), plane_first),
                (FINAL, row_last),
                (FIRST, row_first),
            ):
                for c in range(3):
                    if gains[c] is not None:
                        real, imag = rotate((gains[c], gains[3 + c]), *turn(step))
                        out[0, c, rows, :] = out[0, c, rows, :] + real
                        out[0, 3 + c, rows, :] = out[0, 3 + c, rows, :] + imag

    def term(rows):
        total = None
        for c in range(3):
            value = ft[0, c, rows, :] * at[0, c, rows, :] - ft[0, 3 + c, rows, :] * at[0, 3 + c, rows, :]
            total = value if total is None else total + value
        return total

    for run in range(2):
        for copy in field_loads[run]:
            copy.wait()
        stage_e(0, run)
        stage_h(0, run)
    pl.semaphore_wait(barrier, len(DIRECT) + n_a - 1)
    for run in range(2):
        for kind in DIRECT:
            make(0, run, kind).start()
    for kind in (EY_MSG, PY_MSG):
        pl.semaphore_signal(ready_sem, inc=1, device_id=shifted(kind), device_id_type=MESH)
    perm_load.wait()
    for x in range(CX):
        coef[x] = COURANT / coef[x]
    bulk(0, 0)
    pl.semaphore_wait(ready_sem, 2)
    for run in range(2):
        for kind in CORNERS:
            make(0, run, kind).start()
    bulk(0, 1)
    for copy in spec_loads:
        copy.wait()

    for step in range(STEPS):
        for run in range(2):
            receive(step, run)
            arrive(step, run)
            if step < LAST:
                stage_e(step + 1, run)
                for kind in (CORNER_A, CORNER_B, EX_MSG, EY_MSG):
                    make(step + 1, run, kind).start()
                stage_h(step + 1, run)
                for kind in (PX_MSG, PY_MSG):
                    make(step + 1, run, kind).start()
                bulk(step + 1, run)
        if step == LAST - 1:
            for x in range(1, CX - 1):
                terms[x] = term(slice(CY * x, CY * (x + 1)))

    flat = terms.reshape(CX * CY, NZ)
    flat[FIRST, :] = term(FIRST)
    flat[FINAL, :] = term(FINAL)
    block = lane // CHUNK
    planes = [term(slice(CY * x, CY * (x + 1))) if x in (0, CX - 1) else terms[x] for x in range(CX)]
    for stride in (1, 2, 4):
        low = (block // stride) % 2 == 0
        fresh = list(planes)
        for j in range(GROUPS):
            if (j // stride) % 2 == 0:
                a, b = planes[j], planes[j + stride]
                fresh[j] = jnp.where(low, a, pltpu.roll(b, CHUNK * stride, 1))
                fresh[j + stride] = jnp.where(low, pltpu.roll(a, NZ - CHUNK * stride, 1), b)
        planes = fresh
    for j in range(GROUPS):
        packed[j] = planes[j]

    def share(offset):
        peer = angle_peer(offset)
        return pltpu.make_async_remote_copy(
            src_ref=packed.at[peer["angle"]],
            dst_ref=landed.at[offset],
            send_sem=gsend_sem.at[offset],
            recv_sem=grecv_sem.at[offset],
            device_id=peer,
            device_id_type=MESH,
        )

    for offset in range(1, n_a):
        share(offset).start()
    for step in range(STEPS):
        for run in range(2):
            for kind in range(6):
                make(step, run, kind).wait_send()
    own_tile = me_x * n_y + me_y
    hits = jnp.int32(0)
    for i in range(tiles.shape[0]):
        hits = hits + jnp.where(tiles[i] == own_tile, 1, 0)
    chosen = jnp.full((CY, NZ), hits, jnp.int32) > 0
    total = packed[me_a]
    for offset in range(1, n_a):
        share(offset).wait_recv()
        total = total + landed[offset]
    total = jnp.where(chosen, total * (1.0 / GROUPS), 0.0)
    for j in range(CX):
        moved = total if j == 0 else pltpu.roll(total, NZ - CHUNK * j, 1)
        grad[j] = moved[:, 0:CHUNK]
    for offset in range(1, n_a):
        share(offset).wait_send()


def write_out(ft, at, grad, ft_out, at_out, grad_out, sem):
    copies = [
        pltpu.make_async_copy(src, dst, sem.at[i])
        for i, (src, dst) in enumerate(((ft, ft_out), (at, at_out), (grad, grad_out)))
    ]
    for copy in copies:
        copy.start()
    for copy in copies:
        copy.wait()


def shards(ff, af, fs, as_, perm, phase_table, angle_index, design_tiles):
    f32 = jnp.float32
    hbm = pl.BlockSpec(memory_space=pl.ANY)
    smem = pl.BlockSpec(memory_space=pltpu.SMEM)
    vmem = pl.BlockSpec(memory_space=pltpu.VMEM)
    loads = 2 * 2 * CX + 3
    flat = (1, 6, CX * CY, NZ)
    cells = (1, 6, CX, CY, NZ)
    held = pl.pallas_call(
        kernel,
        out_shape=(pltpu.VMEM(flat, f32), pltpu.VMEM(flat, f32), pltpu.VMEM((CX, CY, CHUNK), f32)),
        in_specs=[hbm] * 5 + [smem] * 3,
        out_specs=(vmem, vmem, vmem),
        scratch_shapes=[
            pltpu.VMEM((2, 6, (CX + 1) * ROWS, NZ), f32),
            pltpu.VMEM((2, 6, (CX + 1) * ROWS, NZ), f32),
            pltpu.VMEM((CX, CY, NZ), f32),
            pltpu.VMEM((8, 8, NZ), f32),
            pltpu.VMEM((CX, CY, NZ), f32),
            pltpu.VMEM((GROUPS, CY, NZ), f32),
            pltpu.VMEM((GROUPS, CY, NZ), f32),
            pltpu.VMEM((STEPS, 2, 2, 4, CY, NZ), f32),
            pltpu.VMEM((STEPS, 2, 2, 4, CX, NZ), f32),
            pltpu.VMEM((STEPS, 2, 2, 2, NZ), f32),
            pltpu.VMEM((STEPS, 2, 2, 4, CY, NZ), f32),
            pltpu.VMEM((STEPS, 2, 2, 4, CX, NZ), f32),
            pltpu.VMEM((STEPS, 2, 2, 2, NZ), f32),
            pltpu.SemaphoreType.DMA((loads,)),
            pltpu.SemaphoreType.DMA((STEPS, 2, 6)),
            pltpu.SemaphoreType.DMA((STEPS, 2, 6)),
            pltpu.SemaphoreType.DMA((GROUPS,)),
            pltpu.SemaphoreType.DMA((GROUPS,)),
            pltpu.SemaphoreType.REGULAR,
        ],
        compiler_params=pltpu.CompilerParams(collective_id=0, has_side_effects=True),
        name="fdtd",
    )(ff, af, fs.reshape(flat), as_.reshape(flat), perm, phase_table.T, angle_index, design_tiles)
    ft, at, grad = pl.pallas_call(
        write_out,
        out_shape=(
            jax.ShapeDtypeStruct(flat, f32),
            jax.ShapeDtypeStruct(flat, f32),
            jax.ShapeDtypeStruct((CX, CY, CHUNK), f32),
        ),
        in_specs=[hbm] * 3,
        out_specs=(hbm,) * 3,
        scratch_shapes=[pltpu.SemaphoreType.DMA((3,))],
        name="write_out",
    )(*(pltpu.with_memory_space_constraint(a, pltpu.VMEM) for a in held))
    return ft.reshape(cells), at.reshape(cells), grad


def solution(mesh):
    in_specs = (
        P("angle", None, "gx", "gy", None),
        P("angle", None, "gx", "gy", None),
        P("angle", None, "gx", "gy", None),
        P("angle", None, "gx", "gy", None),
        P("gx", "gy", None),
        P(),
        P("angle"),
        P(),
    )
    out_specs = (
        P("angle", None, "gx", "gy", None),
        P("angle", None, "gx", "gy", None),
        P("gx", "gy", "angle"),
    )
    return jax.shard_map(shards, mesh=mesh, in_specs=in_specs, out_specs=out_specs, check_vma=False)
```

time: 44.2 us -> 39.8 us (0.900)
  local copies, waits for them, and re-layouts: 3.32 us -> 0 us
  Pallas kernels: 39.4 us -> 38.3 us
    unnamed x7 -> x0, local copies, waits for them, and re-layouts: 3.32 us -> none
    pallas_call x1 -> x2, Pallas kernels: 39.4 us -> 38.3 us  [the longest x1 37.4 us: shards(): pl.pallas_call(kernel, out_shape=(pltpu.VMEM(flat, f32), pltpu.VMEM(flat,...]
where the time goes in v2:
time: 39.8 us; the launch traced here: 39.6 us
  Pallas kernels  38.3 us (96%)
  between operations  1.29 us (3%)
    pallas_call x1, Pallas kernels, shards(): pl.pallas_call(kernel, out_shape=(pltpu.VMEM(flat, f32), pltpu.VMEM(flat,...  37.4 us
    pallas_call x1, Pallas kernels, shards(): pl.pallas_call(write_out, out_shape=(jax.ShapeDtypeStruct(flat, f32), jax...  0.92 us

profile of v2, /device:TPU:1, one launch (start us, length us, event | category | flops | bytes accessed | tf_op | source)
XLA Modules:
  0.0 39.6 jit_solution(30378521998518734)
XLA Ops:
  1.3 37.4 %fdtd.1 = (f32[1,6,128,128]{3,2,1,0:T(8,128)S(1)}, f32[1,6,128,128]{3,2,1,0:T(8,128)S(1)}, f32[8,16,16]{2,1,0:T(8,128)S(1)}) custom-call(f32[1,12,8,16,128]{4,3,2,1,0:T(8,128)} %ff.1, f32[1,12,8,16,128]{4,3,2,1,0:T(8,128)} %af.1, f32[1,6,128,128]{3,2,1,0:T(8,128)} %bitcast.5, f32[1,6,128,128]{3,2,1,0:T(8,128)} %bitcast.6, f32[8,16,128]{2,1,0:T(8,128)} %perm.1, ...), custom_call_target="tpu_custom_call" | custom-call | tf_op jit(solution)/shard_map/fdtd/pallas_call | solution.py:433
  38.7 0.9 %write_out.1 = (f32[1,6,128,128]{3,2,1,0:T(8,128)}, f32[1,6,128,128]{3,2,1,0:T(8,128)}, f32[8,16,16]{2,1,0:T(8,128)}) custom-call(f32[1,6,128,128]{3,2,1,0:T(8,128)S(1)} %get-tuple-element.9.ft, f32[1,6,128,128]{3,2,1,0:T(8,128)S(1)} %get-tuple-element.10.at, f32[8,16,16]{2,1,0:T(8,128)S(1)} %get-tuple-element.11.grad), custom_call_target="tpu_custom_call" | custom-call | tf_op jit(solution)/shard_map/write_out/pallas_call | solution.py:462

commit v3 on v2

--- a/solution.py
+++ b/solution.py
@@ -19,7 +19,7 @@
 
 KINDS = ((1, -1), (-1, 1), (-1, 0), (1, 0), (0, -1), (0, 1))
 CORNER_A, CORNER_B, EX_MSG, PX_MSG, EY_MSG, PY_MSG = range(6)
-DIRECT = (EX_MSG, PX_MSG, EY_MSG, PY_MSG)
+DIRECT = (EY_MSG, PY_MSG, EX_MSG, PX_MSG)
 CORNERS = (CORNER_A, CORNER_B)
 
 E_FIRST = pl.ds(0, CX, stride=ROWS)
@@ -36,10 +36,11 @@
 
 
 def kernel(
-    ff, af, fs, as_, perm, phase, aidx, tiles,
+    ff, af, fs, as_, perm, phase_in, aidx_in, tiles_in,
     ft, at, grad,
     efield, hfield, coef, phs, terms, packed, landed,
     sx, sy, sc, rx, ry, rc,
+    phase, aidx, tiles,
     load_sem, send_sem, recv_sem, gsend_sem, grecv_sem, ready_sem,
 ):
     me_a = lax.axis_index("angle")
@@ -68,6 +69,7 @@
         copy.start()
         return copy
 
+    small_loads = [load(aidx_in, aidx), load(phase_in, phase), load(tiles_in, tiles)]
     field_loads = []
     for run, src in enumerate((ff, af)):
         group = []
@@ -95,6 +97,8 @@
     row_index = lax.broadcasted_iota(jnp.int32, (CY, NZ), 0)
     x_index = lax.broadcasted_iota(jnp.int32, (CX, NZ), 0)
 
+    for copy in small_loads:
+        copy.wait()
     row = aidx[0]
     for axis, (place, last) in enumerate(((me_x, n_x - 1), (me_y, n_y - 1))):
         angle = jnp.full((8, NZ), phase[axis, row], jnp.float32)
@@ -326,8 +330,8 @@
             copy.wait()
         stage_e(0, run)
         stage_h(0, run)
-    pl.semaphore_wait(barrier, len(DIRECT) + n_a - 1)
-    for run in range(2):
+        if run == 0:
+            pl.semaphore_wait(barrier, len(DIRECT) + n_a - 1)
         for kind in DIRECT:
             make(0, run, kind).start()
     for kind in (EY_MSG, PY_MSG):
@@ -350,11 +354,13 @@
             arrive(step, run)
             if step < LAST:
                 stage_e(step + 1, run)
-                for kind in (CORNER_A, CORNER_B, EX_MSG, EY_MSG):
+                for kind in (CORNER_A, CORNER_B, EY_MSG, EX_MSG):
                     make(step + 1, run, kind).start()
                 stage_h(step + 1, run)
-                for kind in (PX_MSG, PY_MSG):
+                for kind in (PY_MSG, PX_MSG):
                     make(step + 1, run, kind).start()
+        if step < LAST:
+            for run in range(2):
                 bulk(step + 1, run)
         if step == LAST - 1:
             for x in range(1, CX - 1):
@@ -388,7 +394,7 @@
             device_id_type=MESH,
         )
 
-    for offset in range(1, n_a):
+    for offset in (4, 3, 5, 2, 6, 1, 7):
         share(offset).start()
     for step in range(STEPS):
         for run in range(2):
@@ -425,15 +431,14 @@
 def shards(ff, af, fs, as_, perm, phase_table, angle_index, design_tiles):
     f32 = jnp.float32
     hbm = pl.BlockSpec(memory_space=pl.ANY)
-    smem = pl.BlockSpec(memory_space=pltpu.SMEM)
     vmem = pl.BlockSpec(memory_space=pltpu.VMEM)
-    loads = 2 * 2 * CX + 3
+    loads = 2 * 2 * CX + 6
     flat = (1, 6, CX * CY, NZ)
     cells = (1, 6, CX, CY, NZ)
     held = pl.pallas_call(
         kernel,
         out_shape=(pltpu.VMEM(flat, f32), pltpu.VMEM(flat, f32), pltpu.VMEM((CX, CY, CHUNK), f32)),
-        in_specs=[hbm] * 5 + [smem] * 3,
+        in_specs=[hbm] * 8,
         out_specs=(vmem, vmem, vmem),
         scratch_shapes=[
             pltpu.VMEM((2, 6, (CX + 1) * ROWS, NZ), f32),
@@ -449,6 +454,9 @@
             pltpu.VMEM((STEPS, 2, 2, 4, CY, NZ), f32),
             pltpu.VMEM((STEPS, 2, 2, 4, CX, NZ), f32),
             pltpu.VMEM((STEPS, 2, 2, 2, NZ), f32),
+            pltpu.SMEM((2, GROUPS), f32),
+            pltpu.SMEM((1,), jnp.int32),
+            pltpu.SMEM(design_tiles.shape, jnp.int32),
             pltpu.SemaphoreType.DMA((loads,)),
             pltpu.SemaphoreType.DMA((STEPS, 2, 6)),
             pltpu.SemaphoreType.DMA((STEPS, 2, 6)),

time: 39.8 us -> 38.5 us (0.967)
  Pallas kernels: 38.3 us -> 37.1 us
    pallas_call x1, Pallas kernels: 37.4 us -> 36.1 us  [shards(): pl.pallas_call(kernel, out_shape=(pltpu.VMEM(flat, f32), pltpu.VMEM(flat,...]
where the time goes in v3:
time: 38.5 us; the launch traced here: 38.3 us
  Pallas kernels  37.1 us (96%)
  between operations  1.29 us (3%)
    pallas_call x1, Pallas kernels, shards(): pl.pallas_call(kernel, out_shape=(pltpu.VMEM(flat, f32), pltpu.VMEM(flat,...  36.1 us
    pallas_call x1, Pallas kernels, shards(): pl.pallas_call(write_out, out_shape=(jax.ShapeDtypeStruct(flat, f32), jax...  0.92 us

profile of v3, /device:TPU:1, one launch (start us, length us, event | category | flops | bytes accessed | tf_op | source)
XLA Modules:
  0.0 38.3 jit_solution(2378296513829966853)
XLA Ops:
  1.3 36.1 %fdtd.1 = (f32[1,6,128,128]{3,2,1,0:T(8,128)S(1)}, f32[1,6,128,128]{3,2,1,0:T(8,128)S(1)}, f32[8,16,16]{2,1,0:T(8,128)S(1)}) custom-call(f32[1,12,8,16,128]{4,3,2,1,0:T(8,128)} %ff.1, f32[1,12,8,16,128]{4,3,2,1,0:T(8,128)} %af.1, f32[1,6,128,128]{3,2,1,0:T(8,128)} %bitcast.5, f32[1,6,128,128]{3,2,1,0:T(8,128)} %bitcast.6, f32[8,16,128]{2,1,0:T(8,128)} %perm.1, ...), custom_call_target="tpu_custom_call" | custom-call | tf_op jit(solution)/shard_map/fdtd/pallas_call | solution.py:438
  37.4 0.9 %write_out.1 = (f32[1,6,128,128]{3,2,1,0:T(8,128)}, f32[1,6,128,128]{3,2,1,0:T(8,128)}, f32[8,16,16]{2,1,0:T(8,128)}) custom-call(f32[1,6,128,128]{3,2,1,0:T(8,128)S(1)} %get-tuple-element.9.ft, f32[1,6,128,128]{3,2,1,0:T(8,128)S(1)} %get-tuple-element.10.at, f32[8,16,16]{2,1,0:T(8,128)S(1)} %get-tuple-element.11.grad), custom_call_target="tpu_custom_call" | custom-call | tf_op jit(solution)/shard_map/write_out/pallas_call | solution.py:470

commit v4 on v3

--- a/solution.py
+++ b/solution.py
@@ -96,20 +96,6 @@
     not_first = lane > 0
     row_index = lax.broadcasted_iota(jnp.int32, (CY, NZ), 0)
     x_index = lax.broadcasted_iota(jnp.int32, (CX, NZ), 0)
-
-    for copy in small_loads:
-        copy.wait()
-    row = aidx[0]
-    for axis, (place, last) in enumerate(((me_x, n_x - 1), (me_y, n_y - 1))):
-        angle = jnp.full((8, NZ), phase[axis, row], jnp.float32)
-        cosine, sine = jnp.cos(angle), jnp.sin(angle)
-        one, zero = jnp.ones_like(cosine), jnp.zeros_like(cosine)
-        ahead = jnp.full((8, NZ), place, jnp.int32) == last
-        behind = jnp.full((8, NZ), place, jnp.int32) == 0
-        phs[4 * axis] = jnp.where(ahead, cosine, one)
-        phs[4 * axis + 1] = jnp.where(ahead, sine, zero)
-        phs[4 * axis + 2] = jnp.where(behind, cosine, one)
-        phs[4 * axis + 3] = jnp.where(behind, -sine, zero)
 
     def phase_pair(which, run, rows):
         c = phs[2 * which, 0:1, :]
@@ -336,6 +322,21 @@
             make(0, run, kind).start()
     for kind in (EY_MSG, PY_MSG):
         pl.semaphore_signal(ready_sem, inc=1, device_id=shifted(kind), device_id_type=MESH)
+
+    for copy in small_loads:
+        copy.wait()
+    row = aidx[0]
+    for axis, (place, last) in enumerate(((me_x, n_x - 1), (me_y, n_y - 1))):
+        angle = jnp.full((8, NZ), phase[axis, row], jnp.float32)
+        cosine, sine = jnp.cos(angle), jnp.sin(angle)
+        one, zero = jnp.ones_like(cosine), jnp.zeros_like(cosine)
+        ahead = jnp.full((8, NZ), place, jnp.int32) == last
+        behind = jnp.full((8, NZ), place, jnp.int32) == 0
+        phs[4 * axis] = jnp.where(ahead, cosine, one)
+        phs[4 * axis + 1] = jnp.where(ahead, sine, zero)
+        phs[4 * axis + 2] = jnp.where(behind, cosine, one)
+        phs[4 * axis + 3] = jnp.where(behind, -sine, zero)
+
     perm_load.wait()
     for x in range(CX):
         coef[x] = COURANT / coef[x]
@@ -354,7 +355,7 @@
             arrive(step, run)
             if step < LAST:
                 stage_e(step + 1, run)
-                for kind in (CORNER_A, CORNER_B, EY_MSG, EX_MSG):
+                for kind in (EY_MSG, CORNER_A, CORNER_B, EX_MSG):
                     make(step + 1, run, kind).start()
                 stage_h(step + 1, run)
                 for kind in (PY_MSG, PX_MSG):

time: 38.5 us -> 38.5 us (level)
  no operation moved by 1% of the time
where the time goes in v4:
time: 38.5 us; the launch traced here: 38.3 us
  Pallas kernels  37.1 us (96%)
  between operations  1.29 us (3%)
    pallas_call x1, Pallas kernels, shards(): pl.pallas_call(kernel, out_shape=(pltpu.VMEM(flat, f32), pltpu.VMEM(flat,...  36.1 us
    pallas_call x1, Pallas kernels, shards(): pl.pallas_call(write_out, out_shape=(jax.ShapeDtypeStruct(flat, f32), jax...  0.92 us

profile of v4, /device:TPU:1, one launch (start us, length us, event | category | flops | bytes accessed | tf_op | source)
XLA Modules:
  0.0 38.3 jit_solution(12471607856154489688)
XLA Ops:
  1.3 36.1 %fdtd.1 = (f32[1,6,128,128]{3,2,1,0:T(8,128)S(1)}, f32[1,6,128,128]{3,2,1,0:T(8,128)S(1)}, f32[8,16,16]{2,1,0:T(8,128)S(1)}) custom-call(f32[1,12,8,16,128]{4,3,2,1,0:T(8,128)} %ff.1, f32[1,12,8,16,128]{4,3,2,1,0:T(8,128)} %af.1, f32[1,6,128,128]{3,2,1,0:T(8,128)} %bitcast.5, f32[1,6,128,128]{3,2,1,0:T(8,128)} %bitcast.6, f32[8,16,128]{2,1,0:T(8,128)} %perm.1, ...), custom_call_target="tpu_custom_call" | custom-call | tf_op jit(solution)/shard_map/fdtd/pallas_call | solution.py:439
  37.4 0.9 %write_out.1 = (f32[1,6,128,128]{3,2,1,0:T(8,128)}, f32[1,6,128,128]{3,2,1,0:T(8,128)}, f32[8,16,16]{2,1,0:T(8,128)}) custom-call(f32[1,6,128,128]{3,2,1,0:T(8,128)S(1)} %get-tuple-element.9.ft, f32[1,6,128,128]{3,2,1,0:T(8,128)S(1)} %get-tuple-element.10.at, f32[8,16,16]{2,1,0:T(8,128)S(1)} %get-tuple-element.11.grad), custom_call_target="tpu_custom_call" | custom-call | tf_op jit(solution)/shard_map/write_out/pallas_call | solution.py:471
